TPU v7x, 32 devices: a whole 2x2x4 slice. The times are simulated.
32 devices in a mesh: row: 4 (over y, core), col: 8 (over z, x).
Axes of the slice: x: 2, y: 2, z: 4, core: 2. Of those that a mesh axis runs over, the one named last changes fastest.
Arguments:
- covariance: float32 [16384, 16384], P('row', 'col'), as said below
- weights: float32 [16384], P(('row', 'col')), may hold values from 0.5 to 1
- dual_slacks: float32 [16384], P(('row', 'col')), may hold values from 2.5 to 10
- returns: float32 [16384], P(('row', 'col')), may hold values from -6 to 6
- targets: float32 [256], P('col'), may hold values from 0.5 to 1
- sector_duals: float32 [256], replicated, may hold values from -6 to 6
- lengths: int32 [256], replicated, may hold values from 1 to 1024, 16384 in all
Outputs:
- factored: float32 [16384, 16384], P('row', 'col')
- solved_rhs: float32 [16384], P('row')
- sector_cols: float32 [16384, 256], P('row', 'col')
- sector_resid: float32 [256], P('col')
Inputs may be any that keep to these rules, and one draw needn't show every extreme that they name: `lengths`: lengths sum to 16384. `covariance`: only the lower triangle with the diagonal is read; with the added diagonal the system is positive definite.
All inputs are finite; a program needn't handle non-finite values.
Results may differ from a plain program's by a relative error of at most 0.0003.
Values sent between devices are 32-bit elements; how exact they have to be, the bound alone decides.
A program may use at most 192 MiB of HBM per device.

v0:
```python
import jax
import jax.numpy as jnp
from jax import lax
from jax.sharding import PartitionSpec as P

NB = 128
PANELS = 8


HIGH = lax.Precision.HIGHEST
SIGMA_GAP = 0.5


def from_root(block, axis, source):
    block = jnp.where(lax.axis_index(axis) == source, block, jnp.zeros_like(block))
    return lax.psum(block, axis)


def lower_inverse(diag_block):
    symmetric = jnp.tril(diag_block) + jnp.tril(diag_block, -1).T
    factor = jnp.linalg.cholesky(symmetric)
    identity = jnp.eye(diag_block.shape[0], dtype=jnp.float32)
    inverse = lax.linalg.triangular_solve(factor, identity, left_side=True, lower=True)
    return (factor, inverse)


def panel_rows(raw_rows, inverse, factor, global_index, panel_first, width):
    computed = jnp.dot(raw_rows, inverse.T, precision=HIGH)
    inside = (global_index >= panel_first) & (global_index < panel_first + width)
    placed = jnp.take(factor, jnp.clip(global_index - panel_first, 0, width - 1), axis=0)
    below_rows = global_index >= panel_first + width
    return jnp.where(below_rows[:, None], computed, jnp.where(inside[:, None], placed, 0.0))


def on_device(covariance, weights, dual_slacks, returns, targets, sector_duals, lengths):
    tile_rows, tile_cols = covariance.shape
    order_total = tile_rows * lax.axis_size("row")
    row_id = lax.axis_index("row")
    col_id = lax.axis_index("col")
    row_start = row_id * tile_rows
    col_start = col_id * tile_cols
    sectors_here = targets.shape[0]
    global_rows = row_start + jnp.arange(tile_rows, dtype=jnp.int32)
    global_cols = col_start + jnp.arange(tile_cols, dtype=jnp.int32)
    full_weights, full_slacks, full_returns = (
        lax.all_gather(weights, ("row", "col"), axis=0, tiled=True),
        lax.all_gather(dual_slacks, ("row", "col"), axis=0, tiled=True),
        lax.all_gather(returns, ("row", "col"), axis=0, tiled=True),
    )
    sector_ends = jnp.cumsum(lengths)
    offsets = sector_ends - lengths
    gap_total = lax.psum(jnp.sum(weights * dual_slacks), ("row", "col"))
    mean_gap = gap_total / order_total
    sector_index = col_id * sectors_here + jnp.arange(sectors_here, dtype=jnp.int32)
    all_assets = jnp.arange(order_total, dtype=jnp.int32)
    local_offsets = jnp.take(offsets, sector_index)
    local_ends = jnp.take(sector_ends, sector_index)
    column_member = (
        (all_assets[None, :] >= local_offsets[:, None])
        & (all_assets[None, :] < local_ends[:, None])
    ).astype(jnp.float32)
    sector_sizes = jnp.take(lengths, sector_index).astype(jnp.float32)
    sector_resid = targets - jnp.dot(column_member, full_weights, precision=HIGH) / sector_sizes
    lower_mask = global_rows[:, None] >= global_cols[None, :]
    strict_mask = global_rows[:, None] > global_cols[None, :]
    weight_rows = lax.dynamic_slice_in_dim(full_weights, row_start, tile_rows)
    weight_cols = lax.dynamic_slice_in_dim(full_weights, col_start, tile_cols)
    row_part = jnp.dot(jnp.where(lower_mask, covariance, 0.0), weight_cols, precision=HIGH)
    col_part = jnp.dot(weight_rows, jnp.where(strict_mask, covariance, 0.0), precision=HIGH)
    partial_value = lax.dynamic_update_slice_in_dim(
        jnp.zeros((order_total,), jnp.float32), row_part, row_start, 0
    )
    partial_value = partial_value + lax.dynamic_update_slice_in_dim(
        jnp.zeros((order_total,), jnp.float32), col_part, col_start, 0
    )
    product = lax.psum(partial_value, ("row", "col"))
    returns_rows = lax.dynamic_slice_in_dim(full_returns, row_start, tile_rows)
    slacks_rows = lax.dynamic_slice_in_dim(full_slacks, row_start, tile_rows)
    row_member = (
        (global_rows[:, None] >= offsets[None, :]) & (global_rows[:, None] < sector_ends[None, :])
    ).astype(jnp.float32)
    price_rows = jnp.dot(row_member, sector_duals, precision=HIGH)
    rhs_rows = (
        returns_rows
        - lax.dynamic_slice_in_dim(product, row_start, tile_rows)
        - price_rows
        + SIGMA_GAP * mean_gap / weight_rows
    )
    sector_rows = (
        lax.dynamic_slice_in_dim(row_member, col_id * sectors_here, sectors_here, 1)
        * lax.rsqrt(sector_sizes)[None, :]
    )
    extras = jnp.concatenate([rhs_rows[:, None], sector_rows], axis=1)
    work = covariance + jnp.where(
        global_rows[:, None] == global_cols[None, :], (slacks_rows / weight_rows)[:, None], 0.0
    )
    slice_root = col_start // tile_rows
    slice_offset = col_start - slice_root * tile_rows
    lead_count = PANELS * NB
    span_cols = min(tile_cols, lead_count)
    pieces = from_root(work[:, :span_cols], "col", 0)
    packed = from_root(
        jnp.concatenate([pieces[:lead_count], extras[:lead_count]], axis=1), "row", 0
    )
    lead_cols = from_root(
        lax.dynamic_slice_in_dim(pieces, slice_offset, tile_cols, 0), "row", slice_root
    )
    factor, inverse = lower_inverse(packed[:, :lead_count])
    rows_factor = panel_rows(pieces, inverse, factor, global_rows, 0, lead_count)
    cols_factor = panel_rows(lead_cols, inverse, factor, global_cols, 0, lead_count)
    solved_head = jnp.dot(inverse, packed[:, lead_count:], precision=HIGH)
    trail_rows = jnp.where((global_rows >= lead_count)[:, None], rows_factor, 0.0)
    trail_cols = jnp.where((global_cols >= lead_count)[:, None], cols_factor, 0.0)
    work = work - lax.dot_general(trail_rows, trail_cols, (((1,), (1,)), ((), ())), precision=HIGH)
    widened = jnp.concatenate([rows_factor, jnp.zeros((tile_rows, tile_cols), jnp.float32)], axis=1)
    lead_part = lax.dynamic_slice_in_dim(widened, jnp.minimum(col_start, lead_count), tile_cols, 1)
    work = jnp.where((global_cols < lead_count)[None, :], lead_part, work)
    inside = global_rows < lead_count
    placed = jnp.take(solved_head, jnp.clip(global_rows, 0, lead_count - 1), axis=0)
    update = jnp.dot(trail_rows, solved_head, precision=HIGH)
    extras = jnp.where(inside[:, None], placed, extras - update)
    factored = jnp.where(lower_mask, work, 0.0)
    return (factored, extras[:, 0], extras[:, 1:], sector_resid)


def solution(mesh):
    return jax.shard_map(
        on_device,
        mesh=mesh,
        in_specs=(
            P("row", "col"),
            P(("row", "col")),
            P(("row", "col")),
            P(("row", "col")),
            P("col"),
            P(),
            P(),
        ),
        out_specs=(P("row", "col"), P("row"), P("row", "col"), P("col")),
        check_vma=False,
    )
```

profile of v0, /device:TPU:0, one launch (start us, length us, event | category | flops | bytes accessed | tf_op | source)
XLA Modules:
  0.0 1734.6 jit_solution(4770853076511306441)
XLA Ops:
  7.3 70.3 %all-gather.1 = f32[32,1,512]{2,1,0:T(1,128)S(1)} all-gather(f32[1,1,512]{2,1,0:T(1,128)} %bitcast.160), channel_id=1, replica_groups=mesh['row'=4,'col'=8] {'row','col'}, dimensions={0}, use_global_device_ids=true | all-gather | bytes 67584 | tf_op jit(solution)/shard_map/all_gather | solution.py:46
  77.6 63.9 %all-gather = f32[32,1,512]{2,1,0:T(1,128)S(1)} all-gather(f32[1,1,512]{2,1,0:T(1,128)} %bitcast.161), channel_id=1, replica_groups=mesh['row'=4,'col'=8] {'row','col'}, dimensions={0}, use_global_device_ids=true | all-gather | bytes 67584 | tf_op jit(solution)/shard_map/all_gather | solution.py:47
  141.5 33.9 %fusion = f32[1,4096]{1,0:T(1,128)S(1)} fusion(f32[2048,1]{0,1:T(1,128)S(1)} %bitcast.157, f32[4096,2048]{1,0:T(8,128)} %param.9, s32[2048]{0:T(1024)S(1)} %iota_add_fusion.1, s32[4096]{0:T(1024)S(1)} %iota_add_fusion), kind=kOutput, calls=%fused_computation.11 | convolution fusion | flops 117440512 | bytes 33603584 | tf_op jit(solution)/shard_map/dot_general | solution.py:68
  175.4 21.6 %fusion.2 = f32[1,2048]{1,0:T(1,128)S(1)} fusion(f32[4096,1]{0,1:T(1,128)S(1)} %bitcast.147, f32[4096,2048]{1,0:T(8,128)} %param.9, s32[2048]{0:T(1024)S(1)} %iota_add_fusion.1, s32[4096]{0:T(1024)S(1)} %iota_add_fusion), kind=kOutput, calls=%fused_computation.13 | convolution fusion | flops 117440512 | bytes 33603584 | tf_op jit(solution)/shard_map/dot_general | solution.py:69
  198.6 13.1 select_add_fusion
  211.7 11.7 copy-done.3
  223.3 6.2 slice_select_fusion
  230.8 37.7 %psum.37 = f32[]{:T(128)} all-reduce(f32[]{:T(128)} %multiply_reduce_fusion), channel_id=1, replica_groups=mesh['row'=4,'col'=8] {'row','col'}, use_global_device_ids=true, to_apply=%region_5.6 | all-reduce | flops 1 | bytes 8 | tf_op jit(solution)/shard_map/psum | solution.py:52
  270.3 66.9 %all-gather.2 = f32[32,1,512]{2,1,0:T(1,128)S(1)} all-gather(f32[1,1,512]{2,1,0:T(1,128)S(1)} %bitcast.162), channel_id=1, replica_groups=mesh['row'=4,'col'=8] {'row','col'}, dimensions={0}, use_global_device_ids=true | all-gather | bytes 67584 | tf_op jit(solution)/shard_map/all_gather | solution.py:48
  340.7 489.7 %all-reduce.7.cloned.1.call-done = f32[4096,1024]{1,0:T(8,128)} async-done(((f32[4096,1024]{1,0:T(8,128)}), f32[4096,1024]{1,0:T(8,128)}) %all-reduce.7.cloned.1.call-update) | async-done | bytes 16777232 | tf_op jit(solution)/shard_map/psum | solution.py:16
  835.3 8.5 dynamic-slice_select_fusion
  846.2 2.7 fusion.68
  850.9 221.2 %all-reduce.11.cloned.1.call-done = (f32[1024,1057]{1,0:T(8,128)}, f32[2048,1024]{1,0:T(8,128)}) async-done(((f32[1024,1057]{1,0:T(8,128)}, f32[2048,1024]{1,0:T(8,128)}), (f32[1024,1057]{1,0:T(8,128)}, f32[2048,1024]{1,0:T(8,128)})) %all-reduce.11.cloned.1.call-update) | async-done | bytes 12718096 | tf_op jit(solution)/shard_map/psum | solution.py:16
  1072.1 4.7 fusion.32
  1076.8 5.4 copy.23
  1082.2 5.9 bitcast_add_fusion.1
  1088.0 5.5 copy.24
  1093.5 4.4 fusion.28
  1099.9 11.7 cholesky.222
  1114.1 9.8 custom-call.62
  1127.9 11.9 cholesky.243
  1140.4 9.8 custom-call.63
  1153.6 11.7 cholesky.466
  1166.6 9.8 custom-call.64
  1180.0 12.1 cholesky.485
  1193.4 9.8 custom-call.65
  1206.7 11.7 cholesky.504
  1219.7 9.9 custom-call.66
  1232.9 11.7 cholesky.524
  1246.0 9.8 custom-call.67
  1258.8 12.1 cholesky.544
  1272.2 9.8 custom-call.68
  1284.6 11.7 cholesky.562
  1303.2 6.6 fusion.31
  1309.8 23.3 %while.1 = (s32[]{:T(128)}, f32[1024,1024]{1,0:T(8,128)}, s32[8,2]{0,1:T(2,128)S(1)}, f32[8,128,128]{2,1,0:T(8,128)S(1)}, s32[]{:T(128)}) while((s32[]{:T(128)}, f32[1024,1024]{1,0:T(8,128)}, s32[8,2]{0,1:T(2,128)S(1)}, f32[8,128,128]{2,1,0:T(8,128)S(1)}, s32[]{:T(128)}) %tuple.71), condition=%wide.while_cond, body=%wide.while_body.sunk | while | flops 2 | bytes 131181 | solution.py:23
  1333.1 78.8 %custom-call.69 = f32[8,128,128]{1,2,0:T(8,128)S(1)} custom-call(f32[8,128,128]{2,1,0:T(8,128)S(1)} %get-tuple-element.12), custom_call_target="InvertDiagBlocksLowerTriangular" | custom-call | tf_op jit(solution)/shard_map/triangular_solve | solution.py:23
  1423.2 2.6 convolution_subtract_fusion.2
  1426.5 2.8 convolution_subtract_fusion.1
  1430.0 3.2 convolution_subtract_fusion.3
  1435.8 5.1 fusion.79
  1441.1 10.8 gather_fusion.2
  1452.5 24.7 %gather_fusion = f32[4096,1024]{1,0:T(8,128)} fusion(f32[1024,1024]{1,0:T(8,128)} %get-tuple-element.32, s32[4096]{0:T(1024)S(1)} %broadcast_clamp_fusion), kind=kCustom, calls=%fused_computation.3 | custom fusion | bytes 33570816 | tf_op jit(solution)/shard_map/jit(_take)/gather | solution.py:30
  1477.2 62.8 %select_select_fusion = f32[4096,1024]{1,0:T(8,128)S(1)} fusion(f32[4096,1024]{1,0:T(8,128)} %gather_fusion, pred[4096]{0:T(1024)(128)(4,1)S(1)} %get-tuple-element.98, pred[4096]{0:T(1024)(128)(4,1)S(1)} %get-tuple-element.99, pred[4096]{0:T(1024)(128)(4,1)S(1)} %fusion.121, f32[4096,1024]{1,0:T(8,128)} %all-reduce.7.cloned.1.call-done, ...), kind=kOutput, calls=%fused_computation.18 | convolution fusion | flops 51552190464 | bytes 54538240 | tf_op jit(solution)/shard_map/dot_general | solution.py:28
  1540.0 18.2 %fusion.25 = f32[4096,33]{0,1:T(8,128)S(1)} fusion(f32[1024,33]{0,1:T(8,128)S(1)} %fusion.79, f32[4096,1024]{1,0:T(8,128)S(1)} %select_select_fusion, pred[4096]{0:T(1024)(128)(4,1)S(1)} %fusion.121, f32[4096,32]{0,1:T(8,128)} %copy-done.9, f32[4096,1]{0,1:T(1,128)S(1)} %bitcast.146, f32[4096,33]{0,1:T(8,128)S(1)} %copy.26, ...), kind=kOutput, calls=%fused_computation.39 | convolution fusion | flops 1665679360 | bytes 18546688 | tf_op jit(solution)/shard_map/dot_general | solution.py:120
  1559.7 30.8 %fusion.145 = f32[2048,1024]{1,0:T(8,128)} fusion(f32[2048,1024]{1,0:T(8,128)} %get-tuple-element.30, f32[1024,1024]{1,0:T(8,128)S(1)} %copy-done.8), kind=kOutput, calls=%fused_computation.266 | convolution fusion | flops 25769803776 | bytes 20971520 | tf_op jit(solution)/shard_map/dot_general | solution.py:28
  1590.4 14.0 gather_fusion.1
  1604.4 6.8 fusion.175
  1611.3 116.4 %compare_select_fusion = f32[4096,2048]{1,0:T(8,128)} fusion(s32[]{:T(128)S(6)} %select_n.176, f32[4096,1024]{1,0:T(8,128)} %copy-done.4, f32[4096,2048]{1,0:T(8,128)} %copy-done.3, s32[2048]{0:T(1024)S(1)} %copy-done.14, s32[4096]{0:T(1024)S(1)} %copy-done.11, pred[2048]{0:T(1024)(128)(4,1)S(1)} %copy-done.18, pred[4096]{0:T(1024)(128)(4,1)S(1)} %fusion.121, ...), kind=kOutput, calls=%fused_computation.9 | convolution fusion | flops 103116963840 | bytes 109082624 | tf_op jit(solution)/shard_map/dot_general | solution.py:114
  (167 shorter events, 93.9 us)
Async XLA Ops:
  7.2 331.2 %copy-start = (f32[256]{0:T(256)S(1)}, f32[256]{0:T(256)}, u32[]{:S(2)}) copy-start(f32[256]{0:T(256)} %param.14) | copy-start | bytes 3076
  7.2 332.5 %all-reduce.9.cloned.1.call-start = ((), (), s32[]{:S(2)}) async-start(), calls=%async_computation.1 | async-start | bytes 131072 | tf_op jit(solution)/shard_map/psum | solution.py:76
  7.2 191.3 %copy-start.13 = (s32[2048]{0:T(1024)}, s32[2048]{0:T(1024)S(1)}, u32[]{:S(2)}) copy-start(s32[2048]{0:T(1024)S(1)} %iota_add_fusion.1) | copy-start | bytes 24580
  7.3 330.2 %copy-start.10 = (s32[4096]{0:T(1024)}, s32[4096]{0:T(1024)S(1)}, u32[]{:S(2)}) copy-start(s32[4096]{0:T(1024)S(1)} %iota_add_fusion) | copy-start | bytes 49156
  197.4 0.6 copy-start.12
  198.0 632.4 %all-reduce.7.cloned.1.call-start = ((), (), s32[]{:S(2)}) async-start(), calls=%async_computation | async-start | bytes 33554432 | tf_op jit(solution)/shard_map/psum | solution.py:16
  211.7 11.7 copy-start.3
  229.5 0.7 copy-start.15
  229.5 0.7 copy-start.16
  229.5 39.0 %copy-start.2 = (s32[256]{0:T(256)S(1)}, s32[256]{0:T(256)}, u32[]{:S(2)}) copy-start(s32[256]{0:T(256)} %param.15) | copy-start | bytes 3076
  229.5 40.8 %copy-start.17 = (f32[512]{0:T(512)S(1)}, f32[512]{0:T(512)}, u32[]{:S(2)}) copy-start(f32[512]{0:T(512)} %param.12) | copy-start | bytes 6148
  229.5 842.6 %all-reduce.11.cloned.1.call-start = ((), (), s32[]{:S(2)}) async-start(), calls=%async_computation.2 | async-start | bytes 26214400 | tf_op jit(solution)/shard_map/psum | solution.py:16
  339.7 490.8 %copy-start.9 = (f32[4096,32]{0,1:T(8,128)}, f32[4096,32]{0,1:T(8,128)S(1)}, u32[]{:S(2)}) copy-start(f32[4096,32]{0,1:T(8,128)S(1)} %convert_multiply_fusion) | copy-start | bytes 1572868
  830.5 2.2 slice-start
  843.8 5.3 copy-start.19
  1098.0 1.9 copy-start.6
  1411.9 3.2 copy-start.5
  1433.8 1.9 copy-start.7
  1540.0 18.2 %copy-start.4 = (f32[4096,1024]{1,0:T(8,128)}, f32[4096,1024]{1,0:T(8,128)S(1)}, u32[]{:S(2)}) copy-start(f32[4096,1024]{1,0:T(8,128)S(1)} %select_select_fusion) | copy-start | bytes 50331652
  1540.0 19.7 %copy-start.8 = (f32[1024,1024]{1,0:T(8,128)S(1)}, f32[1024,1024]{1,0:T(8,128)}, u32[]{:S(2)}) copy-start(f32[1024,1024]{1,0:T(8,128)} %copy-done.7) | copy-start | bytes 12582916
  1604.4 6.8 copy-start.11
  1604.4 6.8 copy-start.14
  1604.4 6.8 copy-start.18
  1611.3 116.4 %copy-start.1 = (f32[256]{0:T(256)S(1)}, f32[256]{0:T(256)}, u32[]{:S(2)}) copy-start(f32[256]{0:T(256)} %param.14) | copy-start | bytes 3076
Sparse Core Ops, SparseCore 0:
  198.1 117.3 all-reduce.8
  319.6 510.7 all-reduce.6
  843.9 228.1 all-reduce.10
where the time goes:
time: 1740 us; the launch traced here: 1730 us
  waiting for transfers between devices  711 us (41%)
  matrix products  337 us (19%)
  other arithmetic  317 us (18%)
  blocking collectives  239 us (14%)
  local copies, waits for them, and re-layouts  110 us (6%)
  between operations  20.4 us (1%)
    psum x2, waiting for transfers between devices, from_root(): return lax.psum(block, axis)  711 us
    another operation x30, other arithmetic, lower_inverse(): factor = jnp.linalg.cholesky(symmetric)  173 us
    dot_general x1, matrix products, on_device(): lax.dot_general(trail_rows, trail_cols, (((1,), (1,)), ((), ())), precisi...  116 us
    dot_general x2, matrix products, panel_rows(): computed = jnp.dot(raw_rows, inverse.T, precision=HIGH)  93.5 us
    another operation x3, other arithmetic, lower_inverse(): lax.linalg.triangular_solve(factor, identity, left_side=True, lower=True)  85.4 us
    all_gather x1, blocking collectives, on_device(): lax.all_gather(weights, ('row', 'col'), axis=0, tiled=True)  70.3 us
    all_gather x1, blocking collectives, on_device(): lax.all_gather(returns, ('row', 'col'), axis=0, tiled=True)  66.9 us
    all_gather x1, blocking collectives, on_device(): lax.all_gather(dual_slacks, ('row', 'col'), axis=0, tiled=True)  63.9 us
  transfers between devices with their start and end apart: 3, of which 2 were waited for; matrix products, arithmetic and copies ran while one was open for 2% of the time, Pallas kernels for 0%

commit v1 on v0

v1 whole, which is shorter than its diff:
```python
import jax
import jax.numpy as jnp
from jax import lax
from jax.experimental import pallas as pl
from jax.experimental.pallas import tpu as pltpu
from jax.sharding import PartitionSpec as P

NB = 128
PANELS = 8


HIGHEST = lax.Precision.HIGHEST
HIGH = lax.Precision.HIGH
SIGMA_GAP = 0.5
NT = (((1,), (1,)), ((), ()))


def eliminate(block):
    width = block.shape[0]
    rows = lax.broadcasted_iota(jnp.int32, (width, width), 0)
    lanes = lax.broadcasted_iota(jnp.int32, (width, width), 1)

    def step(j, carry):
        left, right = carry
        at_row = rows == j
        row = jnp.sum(jnp.where(at_row, left, 0.0), axis=0, keepdims=True)
        other = jnp.sum(jnp.where(at_row, right, 0.0), axis=0, keepdims=True)
        column = jnp.sum(jnp.where(lanes == j, left, 0.0), axis=1, keepdims=True)
        pivot = jnp.sum(jnp.where(lanes[:1] == j, row, 0.0), axis=1, keepdims=True)
        scale = lax.rsqrt(pivot)
        scale = scale * (1.5 - 0.5 * pivot * scale * scale)
        row = row * scale
        other = other * scale
        column = column * scale
        below = rows > j
        left = jnp.where(below, left - column * row, jnp.where(at_row, row, left))
        right = jnp.where(below, right - column * other, jnp.where(at_row, other, right))
        return (left, right)

    identity = (rows == lanes).astype(jnp.float32)
    upper, inverse = lax.fori_loop(0, width, step, (block, identity))
    upper = jnp.where(lanes >= rows, upper, 0.0)
    return (upper.T, inverse)


def factor_kernel(head_ref, factor_ref, inverse_ref):
    order = head_ref.shape[0]
    factor_ref[...] = head_ref[...]
    inverse_ref[...] = jnp.zeros_like(inverse_ref)
    for first in range(0, order, NB):
        last = first + NB
        here = slice(first, last)
        lower, inverse = eliminate(factor_ref[here, here])
        factor_ref[here, here] = lower
        inverse_ref[here, here] = inverse
        if first:
            done = jnp.dot(
                factor_ref[here, :first],
                inverse_ref[:first, :first],
                precision=HIGHEST,
                preferred_element_type=jnp.float32,
            )
            inverse_ref[here, :first] = -jnp.dot(
                inverse, done, precision=HIGHEST, preferred_element_type=jnp.float32
            )
        if last < order:
            below = lax.dot_general(
                factor_ref[last:, here], inverse, NT, precision=HIGHEST,
                preferred_element_type=jnp.float32,
            )
            factor_ref[last:, here] = below
            factor_ref[here, last:] = jnp.zeros((NB, order - last), jnp.float32)
            for top in range(last, order, NB):
                factor_ref[top:, top:top + NB] -= lax.dot_general(
                    below[top - last:], below[top - last:top - last + NB], NT,
                    precision=HIGHEST, preferred_element_type=jnp.float32,
                )


def lower_inverse(symmetric):
    order = symmetric.shape[0]
    shape = jax.ShapeDtypeStruct((order, order), jnp.float32)
    return pl.pallas_call(
        factor_kernel,
        out_shape=(shape, shape),
        in_specs=[pl.BlockSpec(memory_space=pltpu.VMEM)],
        out_specs=(pl.BlockSpec(memory_space=pltpu.VMEM),) * 2,
        compiler_params=pltpu.CompilerParams(vmem_limit_bytes=48 * 1024 * 1024),
        cost_estimate=pl.CostEstimate(
            flops=200 * order**3, bytes_accessed=12 * order * order, transcendentals=order
        ),
    )(symmetric)


def on_device(covariance, weights, dual_slacks, returns, targets, sector_duals, lengths):
    tile_rows, tile_cols = covariance.shape
    row_devices, col_devices = lax.axis_size("row"), lax.axis_size("col")
    order_total = tile_rows * row_devices
    row_id = lax.axis_index("row")
    col_id = lax.axis_index("col")
    row_start = row_id * tile_rows
    col_start = col_id * tile_cols
    sectors_here = targets.shape[0]
    lead = PANELS * NB
    piece = tile_rows // col_devices

    head_raw = jnp.where((row_id == 0) & (col_id == 0), covariance[:lead, :lead], 0.0)
    head_raw = lax.psum(head_raw, ("row", "col"))
    lead_raw = jnp.where(col_id == 0, covariance[:, :lead], 0.0)
    lead_raw = lax.psum_scatter(lead_raw, "col", scatter_dimension=0, tiled=True)

    stacked = jnp.stack([weights, dual_slacks, returns])
    full = lax.all_gather(stacked, ("row", "col"), axis=1, tiled=True)
    full_weights, full_slacks, full_returns = full[0], full[1], full[2]
    full_diag = full_slacks / full_weights

    head = jnp.tril(head_raw)
    symmetric = head + jnp.tril(head_raw, -1).T
    eye = jnp.arange(lead)[:, None] == jnp.arange(lead)[None, :]
    symmetric = symmetric + jnp.where(eye, full_diag[:lead, None], 0.0)
    factor, inverse = lower_inverse(symmetric)

    mine = lax.dot_general(lead_raw, inverse, NT, precision=HIGH)
    piece_id = row_id * col_devices + col_id
    piece_start = piece_id * piece
    padded = jnp.pad(factor, ((0, max(0, piece - lead % piece) if lead % piece else 0), (0, 0)))
    head_rows = lax.dynamic_slice_in_dim(
        padded, jnp.minimum(piece_start, padded.shape[0] - piece), piece
    )
    piece_index = piece_start + jnp.arange(piece, dtype=jnp.int32)
    mine = jnp.where((piece_index < lead)[:, None], head_rows, mine)
    count = row_devices * col_devices
    moves = []
    for source in range(count):
        target_row, target_col = source % row_devices, source // row_devices
        moves.append((source, target_row * col_devices + target_col))
    moved = lax.ppermute(mine, ("row", "col"), moves)
    cols_factor = lax.all_gather(moved, "row", axis=0, tiled=True)
    rows_factor = lax.all_gather(mine, "col", axis=0, tiled=True)

    sector_ends = jnp.cumsum(lengths)
    offsets = sector_ends - lengths
    mean_gap = jnp.sum(full_weights * full_slacks) / order_total
    sector_first = col_id * sectors_here
    local_offsets = lax.dynamic_slice_in_dim(offsets, sector_first, sectors_here)
    local_ends = lax.dynamic_slice_in_dim(sector_ends, sector_first, sectors_here)
    sector_sizes = lax.dynamic_slice_in_dim(lengths, sector_first, sectors_here).astype(jnp.float32)
    all_assets = jnp.arange(order_total, dtype=jnp.int32)
    column_member = (all_assets[None, :] >= local_offsets[:, None]) & (
        all_assets[None, :] < local_ends[:, None]
    )
    held = jnp.sum(jnp.where(column_member, full_weights[None, :], 0.0), axis=1)
    sector_resid = targets - held / sector_sizes

    global_rows = row_start + jnp.arange(tile_rows, dtype=jnp.int32)
    global_cols = col_start + jnp.arange(tile_cols, dtype=jnp.int32)
    lower_mask = global_rows[:, None] >= global_cols[None, :]
    strict_mask = global_rows[:, None] > global_cols[None, :]
    weight_rows = lax.dynamic_slice_in_dim(full_weights, row_start, tile_rows)
    weight_cols = lax.dynamic_slice_in_dim(full_weights, col_start, tile_cols)
    row_part = jnp.sum(jnp.where(lower_mask, covariance * weight_cols[None, :], 0.0), axis=1)
    col_part = jnp.sum(jnp.where(strict_mask, covariance * weight_rows[:, None], 0.0), axis=0)
    zeros = jnp.zeros((order_total,), jnp.float32)
    partial_value = lax.dynamic_update_slice_in_dim(
        zeros, row_part, row_start, 0
    ) + lax.dynamic_update_slice_in_dim(zeros, col_part, col_start, 0)
    partial_value, symmetric = lax.optimization_barrier((partial_value, symmetric))
    product = lax.psum(partial_value, ("row", "col"))

    def right_sides(start, size):
        index = start + jnp.arange(size, dtype=jnp.int32)
        cut = lambda value: lax.dynamic_slice_in_dim(value, start, size)
        member = (index[:, None] >= offsets[None, :]) & (index[:, None] < sector_ends[None, :])
        prices = jnp.sum(jnp.where(member, sector_duals[None, :], 0.0), axis=1)
        rhs = cut(full_returns) - cut(product) - prices + SIGMA_GAP * mean_gap / cut(full_weights)
        local = (index[:, None] >= local_offsets[None, :]) & (index[:, None] < local_ends[None, :])
        columns = local.astype(jnp.float32) * lax.rsqrt(sector_sizes)[None, :]
        return jnp.concatenate([rhs[:, None], columns], axis=1)

    solved_head = jnp.dot(inverse, right_sides(0, lead), precision=HIGHEST)
    extras = right_sides(row_start, tile_rows)

    update = lax.dot_general(rows_factor, cols_factor, NT, precision=HIGH)
    diag_rows = lax.dynamic_slice_in_dim(full_diag, row_start, tile_rows)
    on_diagonal = global_rows[:, None] == global_cols[None, :]
    work = covariance - update + jnp.where(on_diagonal, diag_rows[:, None], 0.0)
    lead_part = jnp.pad(rows_factor, ((0, 0), (0, tile_cols - lead)))
    work = jnp.where((global_cols < lead)[None, :], lead_part, work)
    factored = jnp.where(lower_mask, work, 0.0)

    extras = extras - jnp.dot(rows_factor, solved_head, precision=HIGHEST)
    top = jnp.where(row_id == 0, solved_head, extras[:lead])
    extras = lax.dynamic_update_slice_in_dim(extras, top, 0, 0)
    return (factored, extras[:, 0], extras[:, 1:], sector_resid)


def solution(mesh):
    return jax.shard_map(
        on_device,
        mesh=mesh,
        in_specs=(
            P("row", "col"),
            P(("row", "col")),
            P(("row", "col")),
            P(("row", "col")),
            P("col"),
            P(),
            P(),
        ),
        out_specs=(P("row", "col"), P("row"), P("row", "col"), P("col")),
        check_vma=False,
    )
```

time: 1740 us -> 1030 us (0.59)
  other arithmetic: 317 us -> 52.9 us
  matrix products: 337 us -> 101 us
  blocking collectives: 239 us -> 73.9 us
  Pallas kernels: 0 us -> 165 us
  waiting for transfers between devices: 711 us -> 568 us
  local copies, waits for them, and re-layouts: 110 us -> 32.4 us
    psum x2 -> x1, waiting for transfers between devices: 711 us -> 175 us  [on_device(): head_raw = lax.psum(head_raw, ('row', 'col'))]
    psum x1, waiting for transfers between devices: 0.02 us -> 393 us  [on_device(): product = lax.psum(partial_value, ('row', 'col'))]
    another operation x35 -> x3, other arithmetic: 258 us -> 0.35 us  [the longest x30 173 us: lower_inverse(): factor = jnp.linalg.cholesky(symmetric)]
    dot_general x9 -> x4, matrix products: 292 us -> 101 us  [the longest x1 67.4 us: on_device(): update = lax.dot_general(rows_factor, cols_factor, NT, precision=HIGH)]
    pallas_call x0 -> x1, Pallas kernels: none -> 165 us  [lower_inverse(): pl.pallas_call(factor_kernel, out_shape=(shape, shape), in_specs=[pl.Bloc...]
    all_gather x3 -> x1, blocking collectives: 201 us -> 73.9 us  [on_device(): full = lax.all_gather(stacked, ('row', 'col'), axis=1, tiled=True)]
    gather x7 -> x0, local copies, waits for them, and re-layouts: 52.2 us -> none  [the longest x2 38.6 us: panel_rows(): jnp.take(factor, jnp.clip(global_index - panel_first, 0, width - 1), axis=0)]
    another operation x29 -> x0, matrix products: 45 us -> none  [the longest x14 23.2 us: lower_inverse(): factor = jnp.linalg.cholesky(symmetric)]
  transfers between devices with their start and end apart: 3 -> 6, of which waited for: 2 -> 2; matrix products, arithmetic and copies ran while one was open for 2% -> 10% of each run, Pallas kernels for 0% -> 16%
where the time goes in v1:
time: 1030 us; the launch traced here: 1010 us
  waiting for transfers between devices  568 us (55%)
  Pallas kernels  165 us (16%)
  matrix products  101 us (10%)
  blocking collectives  73.9 us (7%)
  other arithmetic  52.9 us (5%)
  local copies, waits for them, and re-layouts  32.4 us (3%)
  between operations  17 us (2%)
    psum x1, waiting for transfers between devices, on_device(): product = lax.psum(partial_value, ('row', 'col'))  393 us
    psum x1, waiting for transfers between devices, on_device(): head_raw = lax.psum(head_raw, ('row', 'col'))  175 us
    pallas_call x1, Pallas kernels, lower_inverse(): pl.pallas_call(factor_kernel, out_shape=(shape, shape), in_specs=[pl.Bloc...  165 us
    all_gather x1, blocking collectives, on_device(): full = lax.all_gather(stacked, ('row', 'col'), axis=1, tiled=True)  73.9 us
    dot_general x1, matrix products, on_device(): update = lax.dot_general(rows_factor, cols_factor, NT, precision=HIGH)  67.4 us
  transfers between devices with their start and end apart: 6, of which 2 were waited for; matrix products, arithmetic and copies ran while one was open for 10% of the time, Pallas kernels for 16%

profile of v1, /device:TPU:0, one launch (start us, length us, event | category | flops | bytes accessed | tf_op | source)
XLA Modules:
  0.0 1013.5 jit_solution(1934086697790889304)
XLA Ops:
  8.1 4.8 slice.38
  12.8 5.4 copy.32
  18.2 5.0 broadcast_select_fusion
  23.3 12.5 %slice_select_fusion = f32[4096,1024]{1,0:T(8,128)} fusion(f32[4096,2048]{1,0:T(8,128)} %param.7, pred[]{:T(512)S(6)} %eq.13), kind=kLoop, calls=%fused_computation.4 | loop fusion | flops 4194304 | bytes 33554432 | tf_op jit(solution)/shard_map/jit(_where)/select_n | solution.py:109
  35.9 0.6 copy-done.14
  36.5 73.9 %all_gather.9 = f32[3,16384]{1,0:T(4,128)S(1)} all-gather(f32[3,512]{1,0:T(4,128)S(1)} %pad_maximum_fusion), channel_id=1, replica_groups=mesh['row'=4,'col'=8] {'row','col'}, dimensions={1}, use_global_device_ids=true | all-gather | bytes 202752 | tf_op jit(solution)/shard_map/all_gather | solution.py:113
  110.4 0.7 copy-done.2
  111.1 0.8 fusion.14
  111.9 0.6 multiply_reduce_fusion
  112.5 0.6 copy-done.9
  113.2 16.3 %select_reduce_fusion = (f32[2048]{0:T(1024)S(1)}, f32[4096]{0:T(1024)S(1)}) fusion(f32[4096,2048]{1,0:T(8,128)} %param.7, f32[4096]{0:T(1024)S(1)} %bitcast.29, s32[2048]{0:T(1024)S(1)} %iota_add_fusion.1, s32[4096]{0:T(1024)S(1)} %iota_add_fusion, f32[2048]{0:T(1024)S(1)} %bitcast.33), kind=kLoop, calls=%fused_computation.3 | loop fusion | flops 67102720 | bytes 33628160 | tf_op jit(solution)/shard_map/reduce_sum | solution.py:162
  129.6 0.6 broadcast_in_dim.144
  130.2 1.5 dynamic_update_slice.11
  131.7 0.5 add_compare_fusion
  132.2 1.3 add_dynamic-update-slice_fusion
  133.5 174.8 %all-reduce.4.cloned.1.call-done = f32[1024,1024]{0,1:T(8,128)} async-done(((f32[1024,1024]{0,1:T(8,128)}), f32[1024,1024]{0,1:T(8,128)}) %all-reduce.4.cloned.1.call-update) | async-done | bytes 4194320 | tf_op jit(solution)/shard_map/psum | solution.py:108
  308.3 5.4 copy.30
  313.7 6.1 bitcast_add_fusion
  319.7 5.4 copy.31
  325.1 4.8 select_add_fusion.head_ref
  329.9 165.4 %shard_map.102 = (f32[1024,1024]{1,0:T(8,128)S(1)}, f32[1024,1024]{1,0:T(8,128)}) custom-call(f32[1024,1024]{1,0:T(8,128)} %select_add_fusion.head_ref), custom_call_target="tpu_custom_call" | custom-call | flops 214748364800 | bytes 12582912 | tf_op jit(solution)/shard_map/pallas_call | solution.py:83
  495.3 1.9 copy-done
  497.4 8.3 dynamic-slice_select_fusion
  505.8 2.4 collective-permute-start
  508.3 1.3 copy-done.1
  509.7 0.7 dynamic_slice.42
  510.4 0.3 reduce-window.9
  510.7 0.1 slice.44
  510.8 0.1 slice_reduce_fusion
  510.9 0.1 fusion.13
  511.0 0.1 dynamic_slice.48
  511.1 0.1 dynamic_slice.49
  511.8 0.3 select_reduce_fusion.3
  512.1 0.7 select_reduce_fusion.2
  512.8 0.6 divide_subtract_fusion
  513.4 0.8 fusion.15
  514.2 0.1 fusion.9
  514.3 1.3 select_reduce_fusion.1
  515.6 0.7 constant_dynamic-slice_fusion.2
  516.4 0.1 and_select_fusion
  516.5 393.0 %all-reduce.6.cloned.1.call-done = f32[16384]{0:T(1024)} async-done(((f32[16384]{0:T(1024)}), f32[16384]{0:T(1024)}) %all-reduce.6.cloned.1.call-update) | async-done | bytes 65552 | tf_op jit(solution)/shard_map/psum | solution.py:168
  909.5 0.7 fusion.11
  910.2 0.7 divide_add_fusion
  910.9 6.2 fusion.4
  917.2 19.4 %convolution_subtract_fusion = f32[4096,33]{0,1:T(8,128)S(1)} fusion(f32[4096,1024]{1,0:T(8,128)} %all-gather.3.cloned.1.call-done, f32[1024,33]{0,1:T(8,128)S(1)} %fusion.4, f32[4096,32]{0,1:T(8,128)S(1)} %and_select_fusion, f32[4096,1]{0,1:T(1,128)S(1)} %bitcast.31), kind=kOutput, calls=%fused_computation.5 | convolution fusion | flops 1661214720 | bytes 17993728 | tf_op jit(solution)/shard_map/dot_general | solution.py:191
  936.6 0.6 slice.54
  937.2 0.8 slice.55
  938.1 67.4 %compare_select_fusion.1 = f32[4096,2048]{1,0:T(8,128)} fusion(f32[4096,2048]{1,0:T(8,128)} %param.7, f32[4096,1024]{1,0:T(8,128)} %all-gather.3.cloned.1.call-done, f32[2048,1024]{1,0:T(8,128)} %all-gather.5.cloned.1.call-done, f32[4096]{0:T(1024)S(1)} %dynamic_slice.42, s32[2048]{0:T(1024)S(1)} %copy-done.11, s32[4096]{0:T(1024)S(1)} %copy-done.6, ...), kind=kOutput, calls=%fused_computation.1 | convolution fusion | flops 51598327808 | bytes 92317696 | tf_op jit(solution)/shard_map/dot_general | solution.py:183
  (57 shorter events, 0.6 us)
Async XLA Ops:
  8.0 300.3 %all-reduce.4.cloned.1.call-start = ((), (), s32[]{:S(2)}) async-start(), calls=%async_computation.1 | async-start | bytes 8388608 | tf_op jit(solution)/shard_map/psum | solution.py:108
  23.2 474.1 %reduce-scatter.2.cloned.1.call-start = ((), (), s32[]{:S(2)}) async-start(), calls=%async_computation.2 | async-start | bytes 18874368 | tf_op jit(solution)/shard_map/reduce_scatter | solution.py:110
  35.8 0.7 copy-start.14
  35.8 0.7 copy-start.15
  35.8 0.7 copy-start.16
  35.8 873.7 %all-reduce.6.cloned.1.call-start = ((), (), s32[]{:S(2)}) async-start(), calls=%async_computation.5 | async-start | bytes 131072 | tf_op jit(solution)/shard_map/psum | solution.py:168
  110.4 0.7 copy-start.2
  111.9 17.7 %copy-start.3 = (f32[1,16384]{1,0:T(1,128)}, f32[1,16384]{1,0:T(1,128)S(1)}, u32[]{:S(2)}) copy-start(f32[1,16384]{1,0:T(1,128)S(1)} %get-tuple-element.15) | copy-start | bytes 196612
  112.5 0.6 copy-start.9
  113.1 16.4 %copy-start.10 = (s32[2048]{0:T(1024)}, s32[2048]{0:T(1024)S(1)}, u32[]{:S(2)}) copy-start(s32[2048]{0:T(1024)S(1)} %iota_add_fusion.1) | copy-start | bytes 24580
  113.2 16.4 %copy-start.5 = (s32[4096]{0:T(1024)}, s32[4096]{0:T(1024)S(1)}, u32[]{:S(2)}) copy-start(s32[4096]{0:T(1024)S(1)} %iota_add_fusion) | copy-start | bytes 49156
  113.2 16.4 %copy-start.7 = (f32[1,4096]{1,0:T(1,128)}, f32[1,4096]{1,0:T(1,128)S(1)}, u32[]{:S(2)}) copy-start(f32[1,4096]{1,0:T(1,128)S(1)} %constant_dynamic-slice_fusion) | copy-start | bytes 49156
  329.9 167.5 %copy-start.17 = (pred[512]{0:T(512)(128)(4,1)S(1)}, pred[512]{0:T(512)(128)(4,1)}, u32[]{:S(2)}) copy-start(pred[512]{0:T(512)(128)(4,1)} %add_compare_fusion) | copy-start | bytes 1540
  495.3 1.9 copy-start
  497.3 419.9 %all-gather.3.cloned.1.call-start = ((), (), s32[]{:S(2)}) async-start(), calls=%async_computation.3 | async-start | bytes 18874368 | tf_op jit(solution)/shard_map/all_gather | solution.py:139
  505.7 4.7 copy-start.12
  505.7 6.1 copy-start.13
  505.7 6.4 copy-start.4
  505.7 7.0 copy-start.18
  505.7 8.5 copy-start.6
  505.7 404.4 %copy-start.8 = (f32[1,4096]{1,0:T(1,128)S(1)}, f32[1,4096]{1,0:T(1,128)}, u32[]{:S(2)}) copy-start(f32[1,4096]{1,0:T(1,128)} %copy-done.7) | copy-start | bytes 49156
  505.8 432.3 %all-gather.5.cloned.1.call-start = ((), (), s32[]{:S(2)}) async-start(), calls=%async_computation.4 | async-start | bytes 10485760 | tf_op jit(solution)/shard_map/all_gather | solution.py:138
  505.8 2.5 collective-permute-start
  508.3 1.3 copy-start.1
  917.2 20.9 %copy-start.11 = (s32[2048]{0:T(1024)S(1)}, s32[2048]{0:T(1024)}, u32[]{:S(2)}) copy-start(s32[2048]{0:T(1024)} %copy-done.10) | copy-start | bytes 24580
Sparse Core Ops, SparseCore 0:
  23.4 284.8 all-reduce.3
  497.4 412.0 all-reduce.5
Sparse Core Ops, SparseCore 1:
  35.9 304.7 reduce-scatter.1
  505.9 299.9 all-gather.2
  807.3 56.7 all-gather.4
